TPU v7x, 256 devices: a whole 4x4x8 slice. The times are simulated.
256 devices in a mesh: wide: 64 (over y, z, core), narrow: 4 (over x).
Axes of the slice: x: 4, y: 4, z: 8, core: 2. Of those that a mesh axis runs over, the one named last changes fastest.
Arguments:
- patches: bfloat16 [65536, 1280], P('wide', 'narrow'), may hold values from -6 to 6
- norm_gain: float32 [1280], replicated, may hold values from 0.1 to 1.9
- norm_bias: float32 [1280], replicated, may hold values from -3 to 3
- w_in: bfloat16 [1280, 5120], P('wide', 'narrow'), may hold values from -0.15625 to 0.15625
- b_in: float32 [5120], P('narrow'), may hold values from -3 to 3
- w_out: bfloat16 [5120, 1280], P('narrow', 'wide'), may hold values from -0.078125 to 0.078125
- b_out: float32 [1280], P('narrow'), may hold values from -3 to 3
- w_proj: bfloat16 [4, 1280, 1280], P(None, 'narrow', 'wide'), may hold values from -0.078125 to 0.078125
- b_proj: float32 [1280], P('narrow'), may hold values from -3 to 3
- text: bfloat16 [32768, 1280], P('wide', 'narrow'), may hold values from -6 to 6
- place: int32 [16384], replicated, may hold values from -1 to 32767, as said below
Outputs:
- prompt_embeds: bfloat16 [32768, 1280], P('wide', 'narrow')
Inputs may be any that keep to these rules, and one draw needn't show every extreme that they name: `place`: of the 256 entries of one wide index (entries i * 256 to (i + 1) * 256 - 1), the valid ones (>= 0) come first and -1 fills the rest; three quarters or more are valid, and all are valid for some wide index. Valid values are distinct. For one wide index, at most 8 valid entries v have the same v // 512, and every wide index reaches 8 for some value.
All inputs are finite; a program needn't handle non-finite values.
Results may differ from a plain program's by a relative error of at most 0.012.
Values may be sent and summed in bfloat16 or wider, within the bound.
A program may use at most 64 MiB of HBM per device.

v0:
```python
import jax
import jax.numpy as jnp
from jax import lax
from jax.sharding import PartitionSpec as P


def select_rows(index, rows, count):
    pick = (jnp.arange(count, dtype=jnp.int32)[:, None] == index[None, :]).astype(rows.dtype)
    return jnp.dot(pick, rows, preferred_element_type=jnp.float32).astype(rows.dtype)


def per_device(
    patches, norm_gain, norm_bias, w_in, b_in, w_out, b_out, w_proj, b_proj, text, place
):
    groups = lax.axis_size("wide")
    width = w_in.shape[0]
    local = jnp.concatenate([w_in, w_out.T, w_proj.transpose(2, 0, 1).reshape(width, -1)], axis=0)
    gathered = lax.all_gather(local, "wide", axis=0, tiled=False)
    rows_in = gathered[:, :width].reshape(groups * width, -1)
    cols_out = gathered[:, width : 2 * width].reshape(groups * width, -1)
    proj_cols = gathered[:, 2 * width :].reshape(groups * width, -1)
    whole = lax.all_gather(patches, "narrow", axis=1, tiled=True)
    values = whole.astype(jnp.float32)
    center = jnp.mean(values, axis=-1, keepdims=True)
    spread = jnp.mean(jnp.square(values - center), axis=-1, keepdims=True)
    normed = ((values - center) * lax.rsqrt(spread + 1e-06) * norm_gain + norm_bias).astype(
        jnp.bfloat16
    )
    product = jnp.dot(normed, rows_in, preferred_element_type=jnp.float32)
    hidden = jax.nn.gelu(product + b_in, approximate=False).astype(jnp.bfloat16)
    partial_out = lax.dot_general(
        hidden, cols_out, (((1,), (1,)), ((), ())), preferred_element_type=jnp.float32
    )
    mlp_out = lax.psum_scatter(
        partial_out.astype(jnp.bfloat16), "narrow", scatter_dimension=1, tiled=True
    ).astype(jnp.float32)
    stream = (patches.astype(jnp.float32) + (mlp_out + b_out)).astype(jnp.bfloat16)
    merge_count = stream.shape[0] // 4
    merged = stream.reshape(merge_count, 4 * stream.shape[1])
    own_index = lax.axis_index("wide")
    seq_rows = text.shape[0]
    bucket = seq_rows // groups
    place_table = place.reshape(groups, merge_count)
    owners = jnp.where(place_table >= 0, place_table // seq_rows, groups)
    own_owners = lax.dynamic_index_in_dim(owners, own_index, 0, keepdims=False)
    owner_hits = (own_owners[:, None] == jnp.arange(groups, dtype=jnp.int32)[None, :]).astype(
        jnp.int32
    )
    slot_out = jnp.sum(jnp.cumsum(owner_hits, axis=0) * owner_hits, axis=1) - 1
    send_row = jnp.where(
        (own_owners < groups) & (slot_out < bucket), own_owners * bucket + slot_out, -1
    )
    arriving = owners == own_index
    slot_in = jnp.cumsum(arriving.astype(jnp.int32), axis=1) - 1
    slot_in = jnp.where(arriving, slot_in, bucket)
    local_row = place_table % seq_rows
    slot_hits = slot_in[:, :, None] == jnp.arange(bucket, dtype=jnp.int32)[None, None, :]
    targets = jnp.sum(jnp.where(slot_hits, local_row[:, :, None] + 1, 0), axis=1) - 1
    partial_proj = lax.dot_general(
        merged, proj_cols, (((1,), (1,)), ((), ())), preferred_element_type=jnp.float32
    )
    vision = (
        lax.psum_scatter(
            partial_proj.astype(jnp.bfloat16), "narrow", scatter_dimension=1, tiled=True
        ).astype(jnp.float32)
        + b_proj
    ).astype(jnp.bfloat16)
    outgoing = select_rows(send_row, vision, groups * bucket).reshape(groups, bucket, -1)
    received = lax.all_to_all(outgoing, "wide", split_axis=0, concat_axis=0, tiled=True)
    flat_targets = targets.reshape(-1)
    placed = select_rows(flat_targets, received.reshape(-1, received.shape[2]), seq_rows)
    hit = jnp.any(jnp.arange(seq_rows, dtype=jnp.int32)[:, None] == flat_targets[None, :], axis=1)
    return jnp.where(hit[:, None], placed, text)


def solution(mesh):
    placed = (
        P("wide", "narrow"),
        P(),
        P(),
        P("wide", "narrow"),
        P("narrow"),
        P("narrow", "wide"),
        P("narrow"),
        P(None, "narrow", "wide"),
        P("narrow"),
        P("wide", "narrow"),
        P(),
    )
    return jax.shard_map(
        per_device, mesh=mesh, in_specs=placed, out_specs=P("wide", "narrow"), check_vma=False
    )
```

profile of v0, /device:TPU:1, one launch (start us, length us, event | category | flops | bytes accessed | tf_op | source)
XLA Modules:
  0.0 286.6 jit_solution(14069685264983872683)
XLA Ops:
  6.5 0.0 all-gather.5.cloned.1.call-start
  6.5 0.7 all-gather.5.cloned.1.call-update
  7.3 0.0 all-gather.7.cloned.1.call-start
  7.3 0.9 reshape.177
  8.2 1.6 maximum_bitcast_fusion
  9.8 0.0 all-gather.7.cloned.1.call-update
  9.8 0.0 reduce-scatter.5.cloned.1.call-start
  9.9 40.8 %all-gather.5.cloned.1.call-done = bf16[1024,1280]{0,1:T(8,128)(2,1)} async-done(((bf16[1024,320]{0,1:T(8,128)(2,1)}), bf16[1024,1280]{0,1:T(8,128)(2,1)}) %all-gather.5.cloned.1.call-update) | async-done | bytes 2621456 | tf_op jit(solution)/shard_map/all_gather | solution.py:22
  50.7 2.2 convert_reduce_fusion
  52.9 2.5 fusion.2
  55.4 85.1 %all-gather.7.cloned.1.call-done = bf16[64,60,1280]{2,1,0:T(8,128)(2,1)} async-done(((bf16[1,60,1280]{2,1,0:T(8,128)(2,1)}), bf16[64,60,1280]{2,1,0:T(8,128)(2,1)}) %all-gather.7.cloned.1.call-update) | async-done | bytes 9830416 | tf_op jit(solution)/shard_map/all_gather | solution.py:18
  140.5 8.2 %fusion.72 = (bf16[64,20,1280]{2,1,0:T(8,128)(2,1)}, bf16[64,20,1280]{2,1,0:T(8,128)(2,1)}, bf16[64,20,1280]{2,1,0:T(8,128)(2,1)}) fusion(bf16[64,60,1280]{2,1,0:T(8,128)(2,1)} %all-gather.7.cloned.1.call-done), kind=kLoop, calls=%fused_computation.116 | loop fusion | bytes 19660800 | tf_op jit(solution)/shard_map/slice | solution.py:21
  148.7 6.1 %reshape.179 = bf16[1280,1280]{1,0:T(8,128)(2,1)} reshape(bf16[64,20,1280]{2,1,0:T(8,128)(2,1)} %get-tuple-element.6) | data formatting | bytes 6553600 | tf_op jit(solution)/shard_map/reshape | solution.py:20
  154.9 0.0 copy-start
  154.9 0.0 copy-start.3
  154.9 0.0 copy-start.4
  154.9 0.0 copy-start.5
  154.9 6.3 %reshape.178 = bf16[1280,1280]{1,0:T(8,128)(2,1)} reshape(bf16[64,20,1280]{2,1,0:T(8,128)(2,1)} %get-tuple-element.7) | data formatting | bytes 6553600 | tf_op jit(solution)/shard_map/reshape | solution.py:19
  161.2 0.0 copy-done
  161.2 0.0 copy-done.3
  161.2 0.0 copy-done.4
  161.2 0.0 copy-done.5
  161.2 0.0 copy-start.1
  161.2 21.5 %convolution_convert_fusion = bf16[1024,1280]{0,1:T(8,128)(2,1)} fusion(bf16[1280,1280]{1,0:T(8,128)(2,1)} %reshape.179, bf16[1280,1280]{1,0:T(8,128)(2,1)} %reshape.178, bf16[1024,1280]{0,1:T(8,128)(2,1)S(1)} %copy-done, f32[1280]{0:T(1024)S(1)} %copy-done.3, f32[1280]{0:T(1024)S(1)} %copy-done.4, f32[1280]{0:T(1024)S(1)} %copy-done.5, ...), kind=kOutput, calls=%fused_computation.27 | convolution fusion | flops 6806568960 | bytes 11820032 | tf_op jit(solution)/shard_map/dot_general | solution.py:31
  182.7 0.0 copy-start.2
  182.7 0.0 reduce-scatter.5.cloned.1.call-update
  182.7 0.0 reduce-scatter.7.cloned.1.call-start
  182.8 0.0 copy-done.1
  182.8 0.1 fusion.40
  182.9 0.6 reduce-window.14
  183.5 4.6 %reshape.181 = bf16[1280,1280]{1,0:T(8,128)(2,1)S(1)} reshape(bf16[64,20,1280]{2,1,0:T(8,128)(2,1)} %get-tuple-element.5) | data formatting | bytes 6553600 | tf_op jit(solution)/shard_map/reshape | solution.py:21
  188.1 27.8 %reduce-scatter.5.cloned.1.call-done = bf16[1024,320]{0,1:T(8,128)(2,1)} async-done(((bf16[1024,1280]{0,1:T(8,128)(2,1)}), bf16[1024,320]{0,1:T(8,128)(2,1)}) %reduce-scatter.5.cloned.1.call-update) | async-done | bytes 655376 | tf_op jit(solution)/shard_map/reduce_scatter | solution.py:34
  215.9 0.0 copy-done.2
  215.9 2.4 add_convert_fusion
  218.3 0.0 copy-start.6
  218.3 2.2 copy.38
  220.5 2.5 reshape.180
  223.0 3.0 %fusion.21 = bf16[1280,256]{1,0:T(8,128)(2,1)} fusion(bf16[256,1280]{1,0:T(8,128)(2,1)} %reshape.180, bf16[1280,1280]{1,0:T(8,128)(2,1)S(1)} %reshape.181), kind=kOutput, calls=%fused_computation.33 | convolution fusion | flops 839188480 | bytes 4587520 | tf_op jit(solution)/shard_map/dot_general | solution.py:59
  226.0 0.0 reduce-scatter.7.cloned.1.call-update
  226.0 0.2 slice_reduce_fusion.1
  226.3 0.1 fusion.30
  226.4 0.6 reduce-window.16
  227.0 0.2 slice_reduce_fusion
  227.2 0.1 fusion.36
  227.4 21.8 %reduce-scatter.7.cloned.1.call-done = bf16[320,256]{1,0:T(8,128)(2,1)} async-done(((bf16[1280,256]{1,0:T(8,128)(2,1)}), bf16[320,256]{1,0:T(8,128)(2,1)}) %reduce-scatter.7.cloned.1.call-update) | async-done | bytes 163856
  249.1 1.1 copy.42
  250.2 0.0 copy-done.6
  250.2 0.3 convolution_convert_fusion.2
  250.6 0.9 copy.40
  251.5 11.8 %all-to-all-start = ((bf16[64,8,320]{2,1,0:T(8,128)(2,1)}), bf16[64,8,320]{2,1,0:T(8,128)(2,1)S(1)}, u32[]{:S(2)}, u32[]{:S(2)}) async-start(bf16[64,8,320]{2,1,0:T(8,128)(2,1)} %bitcast.9), calls=%async_computation.1 | async-start | bytes 786432 | tf_op jit(solution)/shard_map/all_to_all | solution.py:69
  263.3 1.2 select_reduce_fusion
  264.5 0.1 sub.43
  264.6 0.2 fusion.25
  264.8 13.2 %all-to-all-done = bf16[64,8,320]{2,1,0:T(8,128)(2,1)S(1)} async-done(((bf16[64,8,320]{2,1,0:T(8,128)(2,1)}), bf16[64,8,320]{2,1,0:T(8,128)(2,1)S(1)}, u32[]{:S(2)}, u32[]{:S(2)}) %all-to-all-start) | async-done | bytes 327712 | tf_op jit(solution)/shard_map/all_to_all | solution.py:69
  277.9 2.1 fusion.24
  (12 shorter events, 0.2 us)
Async XLA Ops:
  6.5 44.2 %all-gather.5.cloned.1.call-start = ((), (), s32[]{:S(2)}) async-start(), calls=%async_computation.3 | async-start | bytes 3276800 | tf_op jit(solution)/shard_map/all_gather | solution.py:22
  7.3 133.2 %all-gather.7.cloned.1.call-start = ((), (), s32[]{:S(2)}) async-start(), calls=%async_computation.5 | async-start | bytes 10649600 | tf_op jit(solution)/shard_map/all_gather | solution.py:18
  9.8 206.1 %reduce-scatter.5.cloned.1.call-start = ((), (), s32[]{:S(2)}) async-start(), calls=%async_computation.4 | async-start | bytes 3276800 | tf_op jit(solution)/shard_map/reduce_scatter | solution.py:34
  154.9 6.3 %copy-start = (bf16[1024,1280]{0,1:T(8,128)(2,1)S(1)}, bf16[1024,1280]{0,1:T(8,128)(2,1)}, u32[]{:S(2)}) copy-start(bf16[1024,1280]{0,1:T(8,128)(2,1)} %all-gather.5.cloned.1.call-done) | copy-start | bytes 7864324
  154.9 6.3 %copy-start.3 = (f32[1280]{0:T(1024)S(1)}, f32[1280]{0:T(1024)}, u32[]{:S(2)}) copy-start(f32[1280]{0:T(1024)} %param.15) | copy-start | bytes 15364
  154.9 6.3 %copy-start.4 = (f32[1280]{0:T(1024)S(1)}, f32[1280]{0:T(1024)}, u32[]{:S(2)}) copy-start(f32[1280]{0:T(1024)} %param.13) | copy-start | bytes 15364
  154.9 6.3 %copy-start.5 = (f32[1280]{0:T(1024)S(1)}, f32[1280]{0:T(1024)}, u32[]{:S(2)}) copy-start(f32[1280]{0:T(1024)} %param.12) | copy-start | bytes 15364
  161.2 21.6 %copy-start.1 = (s32[16384]{0:T(1024)S(1)}, s32[16384]{0:T(1024)}, u32[]{:S(2)}) copy-start(s32[16384]{0:T(1024)} %param.21) | copy-start | bytes 196612
  182.7 33.2 %copy-start.2 = (f32[320]{0:T(512)S(1)}, f32[320]{0:T(512)}, u32[]{:S(2)}) copy-start(f32[320]{0:T(512)} %param.17) | copy-start | bytes 3844
  182.7 66.4 %reduce-scatter.7.cloned.1.call-start = ((), (), s32[]{:S(2)}) async-start(), calls=%async_computation.6 | async-start | bytes 819200
  218.3 31.9 %copy-start.6 = (f32[320]{0:T(512)S(1)}, f32[320]{0:T(512)}, u32[]{:S(2)}) copy-start(f32[320]{0:T(512)} %param.19) | copy-start | bytes 3844
  251.5 26.4 %all-to-all-start = ((bf16[64,8,320]{2,1,0:T(8,128)(2,1)}), bf16[64,8,320]{2,1,0:T(8,128)(2,1)S(1)}, u32[]{:S(2)}, u32[]{:S(2)}) async-start(bf16[64,8,320]{2,1,0:T(8,128)(2,1)} %bitcast.9), calls=%async_computation.1 | async-start | bytes 786432 | tf_op jit(solution)/shard_map/all_to_all | solution.py:69
Sparse Core Ops, SparseCore 0:
  9.2 41.5 all-gather.4
  53.5 86.9 all-gather.6
  182.8 33.0 reduce-scatter.4
  226.2 22.9 reduce-scatter.6
where the time goes:
time: 287 us
  waiting for transfers between devices  189 us (66%)
  local copies, waits for them, and re-layouts  33.5 us (12%)
  matrix products  26.9 us (9%)
  between operations  13.3 us (5%)
  starting transfers between devices  12 us (4%)
  other arithmetic  11.6 us (4%)
    all_gather x1, waiting for transfers between devices, per_device(): gathered = lax.all_gather(local, 'wide', axis=0, tiled=False)  85.1 us
    all_gather x1, waiting for transfers between devices, per_device(): whole = lax.all_gather(patches, 'narrow', axis=1, tiled=True)  40.8 us
    reduce_scatter x1, waiting for transfers between devices, per_device(): lax.psum_scatter(partial_out.astype(jnp.bfloat16), 'narrow', scatter_dime...  27.8 us
    unnamed x5, waiting for transfers between devices  22.5 us
    dot_general x1, matrix products, per_device(): lax.dot_general(hidden, cols_out, (((1,), (1,)), ((), ())), preferred_ele...  21.5 us
    all_to_all x1, waiting for transfers between devices, per_device(): lax.all_to_all(outgoing, 'wide', split_axis=0, concat_axis=0, tiled=True)  13.2 us
    all_to_all x1, starting transfers between devices, per_device(): lax.all_to_all(outgoing, 'wide', split_axis=0, concat_axis=0, tiled=True)  11.8 us
    slice x1, local copies, waits for them, and re-layouts, per_device(): proj_cols = gathered[:, 2 * width:].reshape(groups * width, -1)  8.25 us
  transfers between devices with their start and end apart: 5, of which 5 were waited for; matrix products, arithmetic and copies ran while one was open for 5% of the time, Pallas kernels for 0%

commit v1 on v0

--- a/solution.py
+++ b/solution.py
@@ -19,7 +19,9 @@
     rows_in = gathered[:, :width].reshape(groups * width, -1)
     cols_out = gathered[:, width : 2 * width].reshape(groups * width, -1)
     proj_cols = gathered[:, 2 * width :].reshape(groups * width, -1)
-    whole = lax.all_gather(patches, "narrow", axis=1, tiled=True)
+    world_n = lax.axis_size("narrow")
+    y_new = jnp.tile(patches, [world_n if pp == 1 else 1 for pp in range(patches.ndim)])
+    whole = lax.all_to_all(y_new, axis_name="narrow", split_axis=1, concat_axis=1, tiled=True)
     values = whole.astype(jnp.float32)
     center = jnp.mean(values, axis=-1, keepdims=True)
     spread = jnp.mean(jnp.square(values - center), axis=-1, keepdims=True)

time: 287 us -> 245 us (0.85)
  waiting for transfers between devices: 189 us -> 143 us
  starting transfers between devices: 12 us -> 17 us
    all_gather x1 -> x0, waiting for transfers between devices: 40.8 us -> none  [per_device(): whole = lax.all_gather(patches, 'narrow', axis=1, tiled=True)]
    all_gather x1, waiting for transfers between devices: 85.1 us -> 50.6 us  [per_device(): gathered = lax.all_gather(local, 'wide', axis=0, tiled=False)]
    all_to_all x0 -> x1, waiting for transfers between devices: none -> 29.8 us  [per_device(): lax.all_to_all(y_new, axis_name='narrow', split_axis=1, concat_axis=1, ti...]
    all_to_all x0 -> x1, starting transfers between devices: none -> 4.84 us  [per_device(): lax.all_to_all(y_new, axis_name='narrow', split_axis=1, concat_axis=1, ti...]
    another operation x3 -> x4, local copies, waits for them, and re-layouts: 0.19 us -> 3.13 us  [the longest x1 2.94 us: per_device(): jnp.tile(patches, [world_n if pp == 1 else 1 for pp in range(patches.ndim)])]
    unnamed x5 -> x4, waiting for transfers between devices: 22.5 us -> 21.7 us
  transfers between devices with their start and end apart: 5 -> 5, of which waited for: 5 -> 5; matrix products, arithmetic and copies ran while one was open for 5% -> 6% of each run, Pallas kernels for 0% -> 0%
where the time goes in v1:
time: 245 us; the launch traced here: 244 us
  waiting for transfers between devices  143 us (58%)
  local copies, waits for them, and re-layouts  35 us (14%)
  matrix products  25.8 us (11%)
  starting transfers between devices  17 us (7%)
  between operations  13.3 us (5%)
  other arithmetic  10.2 us (4%)
    all_gather x1, waiting for transfers between devices, per_device(): gathered = lax.all_gather(local, 'wide', axis=0, tiled=False)  50.6 us
    all_to_all x1, waiting for transfers between devices, per_device(): lax.all_to_all(y_new, axis_name='narrow', split_axis=1, concat_axis=1, ti...  29.8 us
    reduce_scatter x1, waiting for transfers between devices, per_device(): lax.psum_scatter(partial_out.astype(jnp.bfloat16), 'narrow', scatter_dime...  27.6 us
    unnamed x4, waiting for transfers between devices  21.7 us
    dot_general x1, matrix products, per_device(): lax.dot_general(hidden, cols_out, (((1,), (1,)), ((), ())), preferred_ele...  20.4 us
    all_to_all x1, waiting for transfers between devices, per_device(): lax.all_to_all(outgoing, 'wide', split_axis=0, concat_axis=0, tiled=True)  13.2 us
    all_to_all x1, starting transfers between devices, per_device(): lax.all_to_all(outgoing, 'wide', split_axis=0, concat_axis=0, tiled=True)  11.9 us
    slice x1, local copies, waits for them, and re-layouts, per_device(): proj_cols = gathered[:, 2 * width:].reshape(groups * width, -1)  8.25 us
  transfers between devices with their start and end apart: 5, of which 5 were waited for; matrix products, arithmetic and copies ran while one was open for 6% of the time, Pallas kernels for 0%

profile of v1, /device:TPU:1, one launch (start us, length us, event | category | flops | bytes accessed | tf_op | source)
XLA Modules:
  0.0 244.1 jit_solution(5724253733131913061)
XLA Ops:
  6.5 0.0 copy-start.1
  6.5 0.0 copy-start.2
  6.5 0.0 all-gather.4.cloned.1.call-start
  6.5 1.0 reshape.210
  7.5 1.6 maximum_bitcast_fusion
  9.1 0.0 all-gather.4.cloned.1.call-update
  9.1 2.9 %tile.2 = bf16[1024,4,320]{0,2,1:T(8,128)(2,1)} broadcast(bf16[1024,320]{0,1:T(8,128)(2,1)} %param.11), dimensions={0,2} | broadcast | bytes 3276800 | tf_op jit(solution)/shard_map/tile | solution.py:23
  12.0 4.8 %all-to-all-start = ((bf16[1024,4,320]{0,2,1:T(8,128)(2,1)}), bf16[1024,4,320]{0,2,1:T(8,128)(2,1)S(1)}, u32[]{:S(2)}, u32[]{:S(2)}) async-start(bf16[1024,4,320]{0,2,1:T(8,128)(2,1)} %tile.2), calls=%async_computation | async-start | bytes 5242880 | tf_op jit(solution)/shard_map/all_to_all | solution.py:24
  16.9 0.0 reduce-scatter.5.cloned.1.call-start
  16.9 0.0 copy-done.1
  16.9 0.1 add.116
  17.0 0.0 copy-done.2
  17.0 0.1 mul.46
  17.0 29.8 %all-to-all-done = bf16[1024,4,320]{0,2,1:T(8,128)(2,1)S(1)} async-done(((bf16[1024,4,320]{0,2,1:T(8,128)(2,1)}), bf16[1024,4,320]{0,2,1:T(8,128)(2,1)S(1)}, u32[]{:S(2)}, u32[]{:S(2)}) %all-to-all-start) | async-done | bytes 2621472 | tf_op jit(solution)/shard_map/all_to_all | solution.py:24
  46.8 0.5 convert_reduce_fusion
  47.3 0.7 fusion.2
  48.0 2.1 fusion.5
  50.2 50.6 %all-gather.4.cloned.1.call-done = bf16[64,60,1280]{2,1,0:T(8,128)(2,1)} async-done(((bf16[1,60,1280]{2,1,0:T(8,128)(2,1)}), bf16[64,60,1280]{2,1,0:T(8,128)(2,1)}) %all-gather.4.cloned.1.call-update) | async-done | bytes 9830416 | tf_op jit(solution)/shard_map/all_gather | solution.py:18
  100.8 8.2 %fusion.65 = (bf16[64,20,1280]{2,1,0:T(8,128)(2,1)}, bf16[64,20,1280]{2,1,0:T(8,128)(2,1)}, bf16[64,20,1280]{2,1,0:T(8,128)(2,1)}) fusion(bf16[64,60,1280]{2,1,0:T(8,128)(2,1)} %all-gather.4.cloned.1.call-done), kind=kLoop, calls=%fused_computation.112 | loop fusion | bytes 19660800 | tf_op jit(solution)/shard_map/slice | solution.py:21
  109.1 4.6 %reshape.212 = bf16[1280,1280]{1,0:T(8,128)(2,1)S(1)} reshape(bf16[64,20,1280]{2,1,0:T(8,128)(2,1)} %get-tuple-element.6) | data formatting | bytes 6553600 | tf_op jit(solution)/shard_map/reshape | solution.py:20
  113.7 0.0 copy-start.4
  113.7 6.1 %reshape.211 = bf16[1280,1280]{1,0:T(8,128)(2,1)} reshape(bf16[64,20,1280]{2,1,0:T(8,128)(2,1)} %get-tuple-element.7) | data formatting | bytes 6553600 | tf_op jit(solution)/shard_map/reshape | solution.py:19
  119.8 0.0 copy-done.4
  119.8 0.0 copy-start
  119.8 20.4 %convolution_convert_fusion = bf16[1024,1280]{0,1:T(8,128)(2,1)} fusion(bf16[1280,1280]{1,0:T(8,128)(2,1)S(1)} %reshape.212, bf16[1024,1280]{0,1:T(8,128)(2,1)} %bitcast.42, bf16[1280,1280]{1,0:T(8,128)(2,1)} %reshape.211, f32[1280]{0:T(1024)S(1)} %copy-done.4), kind=kOutput, calls=%fused_computation.27 | convolution fusion | flops 6798704640 | bytes 11801600 | tf_op jit(solution)/shard_map/dot_general | solution.py:33
  140.2 0.0 copy-start.3
  140.2 0.0 reduce-scatter.5.cloned.1.call-update
  140.2 0.2 reduce-scatter.7.cloned.1.call-start
  140.5 0.0 copy-done
  140.5 0.1 fusion.33
  140.6 0.6 reduce-window.14
  141.2 4.6 %reshape.214 = bf16[1280,1280]{1,0:T(8,128)(2,1)S(1)} reshape(bf16[64,20,1280]{2,1,0:T(8,128)(2,1)} %get-tuple-element.5) | data formatting | bytes 6553600 | tf_op jit(solution)/shard_map/reshape | solution.py:21
  145.8 27.6 %reduce-scatter.5.cloned.1.call-done = bf16[1024,320]{0,1:T(8,128)(2,1)} async-done(((bf16[1024,1280]{0,1:T(8,128)(2,1)}), bf16[1024,320]{0,1:T(8,128)(2,1)}) %reduce-scatter.5.cloned.1.call-update) | async-done | bytes 655376 | tf_op jit(solution)/shard_map/reduce_scatter | solution.py:36
  173.5 0.0 copy-done.3
  173.5 2.4 add_convert_fusion
  175.8 0.0 copy-start.5
  175.8 2.2 copy.39
  178.1 2.5 %reshape.213 = bf16[256,1280]{1,0:T(8,128)(2,1)} reshape(bf16[1024,320]{1,0:T(8,128)(2,1)} %copy.39) | data formatting | bytes 1310720 | tf_op jit(solution)/shard_map/reshape | solution.py:41
  180.6 3.0 %fusion.16 = bf16[1280,256]{1,0:T(8,128)(2,1)} fusion(bf16[256,1280]{1,0:T(8,128)(2,1)} %reshape.213, bf16[1280,1280]{1,0:T(8,128)(2,1)S(1)} %reshape.214), kind=kOutput, calls=%fused_computation.29 | convolution fusion | flops 839188480 | bytes 4587520 | tf_op jit(solution)/shard_map/dot_general | solution.py:61
  183.6 0.0 reduce-scatter.7.cloned.1.call-update
  183.6 0.2 slice_reduce_fusion.1
  183.8 0.1 fusion.23
  183.9 0.6 reduce-window.16
  184.6 0.2 slice_reduce_fusion
  184.8 0.1 fusion.29
  184.9 21.7 %reduce-scatter.7.cloned.1.call-done = bf16[320,256]{1,0:T(8,128)(2,1)} async-done(((bf16[1280,256]{1,0:T(8,128)(2,1)}), bf16[320,256]{1,0:T(8,128)(2,1)}) %reduce-scatter.7.cloned.1.call-update) | async-done | bytes 163856
  206.6 1.1 copy.43
  207.7 0.0 copy-done.5
  207.7 0.3 convolution_convert_fusion.2
  208.1 0.9 copy.41
  209.0 11.9 %all-to-all-start.1 = ((bf16[64,8,320]{2,1,0:T(8,128)(2,1)}), bf16[64,8,320]{2,1,0:T(8,128)(2,1)S(1)}, u32[]{:S(2)}, u32[]{:S(2)}) async-start(bf16[64,8,320]{2,1,0:T(8,128)(2,1)} %bitcast.10), calls=%async_computation.2 | async-start | bytes 786432 | tf_op jit(solution)/shard_map/all_to_all | solution.py:71
  220.9 1.2 select_reduce_fusion
  222.0 0.1 sub.45
  222.1 0.2 fusion.18
  222.3 13.2 %all-to-all-done.1 = bf16[64,8,320]{2,1,0:T(8,128)(2,1)S(1)} async-done(((bf16[64,8,320]{2,1,0:T(8,128)(2,1)}), bf16[64,8,320]{2,1,0:T(8,128)(2,1)S(1)}, u32[]{:S(2)}, u32[]{:S(2)}) %all-to-all-start.1) | async-done | bytes 327712 | tf_op jit(solution)/shard_map/all_to_all | solution.py:71
  235.5 2.1 fusion.17
  (12 shorter events, 0.2 us)
Async XLA Ops:
  6.5 10.3 %copy-start.1 = (f32[1280]{0:T(1024)S(1)}, f32[1280]{0:T(1024)}, u32[]{:S(2)}) copy-start(f32[1280]{0:T(1024)} %param.13) | copy-start | bytes 15364
  6.5 10.4 %copy-start.2 = (f32[1280]{0:T(1024)S(1)}, f32[1280]{0:T(1024)}, u32[]{:S(2)}) copy-start(f32[1280]{0:T(1024)} %param.12) | copy-start | bytes 15364
  6.5 94.3 %all-gather.4.cloned.1.call-start = ((), (), s32[]{:S(2)}) async-start(), calls=%async_computation.5 | async-start | bytes 10649600 | tf_op jit(solution)/shard_map/all_gather | solution.py:18
  12.0 34.8 %all-to-all-start = ((bf16[1024,4,320]{0,2,1:T(8,128)(2,1)}), bf16[1024,4,320]{0,2,1:T(8,128)(2,1)S(1)}, u32[]{:S(2)}, u32[]{:S(2)}) async-start(bf16[1024,4,320]{0,2,1:T(8,128)(2,1)} %tile.2), calls=%async_computation | async-start | bytes 5242880 | tf_op jit(solution)/shard_map/all_to_all | solution.py:24
  16.9 156.6 %reduce-scatter.5.cloned.1.call-start = ((), (), s32[]{:S(2)}) async-start(), calls=%async_computation.4 | async-start | bytes 3276800 | tf_op jit(solution)/shard_map/reduce_scatter | solution.py:36
  113.7 6.1 %copy-start.4 = (f32[1280]{0:T(1024)S(1)}, f32[1280]{0:T(1024)}, u32[]{:S(2)}) copy-start(f32[1280]{0:T(1024)} %param.15) | copy-start | bytes 15364
  119.8 20.6 %copy-start = (s32[16384]{0:T(1024)S(1)}, s32[16384]{0:T(1024)}, u32[]{:S(2)}) copy-start(s32[16384]{0:T(1024)} %param.21) | copy-start | bytes 196612
  140.2 33.3 %copy-start.3 = (f32[320]{0:T(512)S(1)}, f32[320]{0:T(512)}, u32[]{:S(2)}) copy-start(f32[320]{0:T(512)} %param.17) | copy-start | bytes 3844
  140.2 66.4 %reduce-scatter.7.cloned.1.call-start = ((), (), s32[]{:S(2)}) async-start(), calls=%async_computation.6 | async-start | bytes 819200
  175.8 31.9 %copy-start.5 = (f32[320]{0:T(512)S(1)}, f32[320]{0:T(512)}, u32[]{:S(2)}) copy-start(f32[320]{0:T(512)} %param.19) | copy-start | bytes 3844
  209.0 26.5 %all-to-all-start.1 = ((bf16[64,8,320]{2,1,0:T(8,128)(2,1)}), bf16[64,8,320]{2,1,0:T(8,128)(2,1)S(1)}, u32[]{:S(2)}, u32[]{:S(2)}) async-start(bf16[64,8,320]{2,1,0:T(8,128)(2,1)} %bitcast.10), calls=%async_computation.2 | async-start | bytes 786432 | tf_op jit(solution)/shard_map/all_to_all | solution.py:71
Sparse Core Ops, SparseCore 0:
  10.1 90.6 all-gather.3
  140.3 33.0 reduce-scatter.4
  183.7 22.8 reduce-scatter.6
